TPU v7x, 32 devices: a whole 2x2x4 slice. The times are simulated.
32 devices in a mesh: row: 4 (over y, core), col: 8 (over z, x).
Axes of the slice: x: 2, y: 2, z: 4, core: 2. Of those that a mesh axis runs over, the one named last changes fastest.
Arguments:
- gradient: bfloat16 [3584, 12288], P('row', 'col'), may hold values from -54 to 54
- momentum: float32 [3584, 12288], P('row', 'col'), may hold values from -54 to 54
Outputs:
- update_matrix: bfloat16 [3584, 12288], P('row', 'col')
- new_momentum: float32 [3584, 12288], P('row', 'col')
All inputs are finite; a program needn't handle non-finite values.
Results may differ from a plain program's by a relative error of at most 0.013.
Values may be sent and summed in bfloat16 or wider, within the bound.
A program may use at most 128 MiB of HBM per device.

v0:
```python
import math

import jax
import jax.numpy as jnp
from jax import lax
from jax.sharding import PartitionSpec as P

M = 3584
N = 12288
ITERS = 2


MOMENTUM_DECAY = 0.95
EPSILON = 1e-07
COEF_LINEAR = 3.4445
COEF_CUBIC = -4.775
COEF_QUINTIC = 2.0315


def passed_along(shard, axis, by):
    count = lax.axis_size(axis)
    return lax.ppermute(shard, axis, [(i, (i + by) % count) for i in range(count)])


def outer_rows(left, right):
    return lax.dot_general(
        left, right, (((1,), (1,)), ((), ())), preferred_element_type=jnp.float32
    )


def per_device(gradient, momentum):
    row_count = lax.axis_size("row")
    grad32 = gradient.astype(jnp.float32)
    buffer = MOMENTUM_DECAY * momentum + grad32
    nesterov = grad32 + MOMENTUM_DECAY * buffer
    iterate = nesterov.astype(jnp.bfloat16)
    block_rows = iterate.shape[0]
    row_index = lax.axis_index("row")
    halfway = row_count // 2
    combined = iterate.astype(jnp.float32)
    for iteration in range(ITERS):
        panel = lax.all_gather(iterate, "row", axis=0, tiled=True)
        rolled = jnp.roll(panel, -row_index * block_rows, axis=0)
        nearby = rolled[: (halfway + 1) * block_rows]
        partial_value = outer_rows(iterate, nearby)
        shares = lax.psum_scatter(
            partial_value.astype(jnp.bfloat16), "col", scatter_dimension=1, tiled=True
        ).astype(jnp.float32)
        width = shares.shape[1]
        column_ids = lax.axis_index("col") * width + jnp.arange(width, dtype=jnp.int32)
        block_ids = column_ids // block_rows
        weights = jnp.where((block_ids == 0) | (block_ids == halfway), 1.0, 2.0).astype(
            jnp.float32
        )[None, :]
        if iteration == 0:
            quartic = lax.psum(jnp.sum(weights * shares * shares), ("row", "col"))
            scale = 1.0 / jnp.sqrt(jnp.sqrt(quartic) + EPSILON)
            shares = shares * (scale * scale)
            iterate = (iterate.astype(jnp.float32) * scale).astype(jnp.bfloat16)
            panel = (panel.astype(jnp.float32) * scale).astype(jnp.bfloat16)
        upper = lax.all_gather(shares.astype(jnp.bfloat16), "col", axis=1, tiled=True)
        pieces = [upper]
        for position in range(halfway + 1, row_count):
            offset = row_count - position
            mirror = upper[:, offset * block_rows : (offset + 1) * block_rows].T
            pieces.append(passed_along(mirror, "row", offset))
        gram = jnp.concatenate(pieces, axis=1)
        ordered = jnp.roll(panel, -row_index * block_rows, axis=0)
        product = jnp.dot(gram, ordered, preferred_element_type=jnp.float32)
        product_panel = lax.all_gather(product.astype(jnp.bfloat16), "row", axis=0, tiled=True)
        product_panel = jnp.roll(product_panel, -row_index * block_rows, axis=0)
        second = jnp.dot(gram, product_panel, preferred_element_type=jnp.float32)
        combined = (
            COEF_LINEAR * iterate.astype(jnp.float32) + COEF_CUBIC * product + COEF_QUINTIC * second
        )
        if iteration + 1 < ITERS:
            iterate = combined.astype(jnp.bfloat16)
    update_matrix = (combined * (0.2 * math.sqrt(max(M, N)))).astype(jnp.bfloat16)
    return (update_matrix, buffer)


def solution(mesh):
    return jax.shard_map(
        per_device,
        mesh=mesh,
        in_specs=(P("row", "col"), P("row", "col")),
        out_specs=(P("row", "col"), P("row", "col")),
        check_vma=False,
    )
```

profile of v0, /device:TPU:0, one launch (start us, length us, event | category | flops | bytes accessed | tf_op | source)
XLA Modules:
  0.0 882.2 jit_solution(1614030632824795732)
XLA Ops:
  7.2 7.9 fusion.15
  15.2 76.0 %all-gather.7.cloned.1.call-done = bf16[3584,1536]{1,0:T(8,128)(2,1)} async-done(((bf16[896,1536]{1,0:T(8,128)(2,1)}), bf16[3584,1536]{1,0:T(8,128)(2,1)}) %all-gather.7.cloned.1.call-update) | async-done | bytes 11010064 | tf_op jit(solution)/shard_map/all_gather | solution.py:42
  91.2 15.5 %fusion.16 = bf16[896,2688]{0,1:T(8,128)(2,1)} fusion(bf16[896,1536]{1,0:T(8,128)(2,1)} %get-tuple-element.3, s32[]{:T(128)S(6)} %select_n.38, bf16[3584,1536]{1,0:T(8,128)(2,1)} %all-gather.7.cloned.1.call-done), kind=kOutput, calls=%fused_computation.28 | convolution fusion | flops 7417675776 | bytes 18579460 | tf_op jit(solution)/shard_map/dot_general | solution.py:26
  106.8 97.2 %reduce-scatter.3.cloned.1.call-done = bf16[896,336]{0,1:T(8,128)(2,1)} async-done(((bf16[896,2688]{0,1:T(8,128)(2,1)}), bf16[896,336]{0,1:T(8,128)(2,1)}) %reduce-scatter.3.cloned.1.call-update) | async-done | bytes 602128 | tf_op jit(solution)/shard_map/reduce_scatter | solution.py:46
  204.0 2.2 fusion.27
  206.1 39.7 %psum.7 = f32[]{:T(128)} all-reduce(f32[]{:T(128)} %fusion.27), channel_id=1, replica_groups=mesh['row'=4,'col'=8] {'row','col'}, use_global_device_ids=true, to_apply=%region_2.4 | all-reduce | flops 1 | bytes 8 | tf_op jit(solution)/shard_map/psum | solution.py:56
  248.7 80.7 %all-gather.9.cloned.1.call-done = bf16[896,2688]{0,1:T(8,128)(2,1)} async-done(((bf16[896,336]{0,1:T(8,128)(2,1)}), bf16[896,2688]{0,1:T(8,128)(2,1)}) %all-gather.9.cloned.1.call-update) | async-done | bytes 4816912 | tf_op jit(solution)/shard_map/all_gather | solution.py:61
  332.7 6.7 multiply_convert_fusion
  339.5 2.6 constant_dynamic-update-slice_fusion.1
  342.1 10.9 %collective-permute-done = bf16[896,896]{0,1:T(8,128)(2,1)S(1)} collective-permute-done((bf16[896,896]{0,1:T(8,128)(2,1)S(1)}, bf16[896,896]{0,1:T(8,128)(2,1)S(1)}, u32[]{:S(2)}, u32[]{:S(2)}) %collective-permute-start) | collective-permute-done | bytes 1605664 | tf_op jit(solution)/shard_map/ppermute | solution.py:22
  354.2 18.2 %fusion.37 = (bf16[896,1536]{1,0:T(8,128)(2,1)}, f32[896,1536]{1,0:T(8,128)}) fusion(bf16[896,3584]{0,1:T(8,128)(2,1)} %constant_dynamic-update-slice_fusion, s32[]{:T(128)S(6)} %select_n.38, bf16[3584,1536]{1,0:T(8,128)(2,1)S(1)} %multiply_convert_fusion), kind=kOutput, calls=%fused_computation.52 | convolution fusion | flops 9888399360 | bytes 25690116 | tf_op jit(solution)/shard_map/dot_general | solution.py:69
  372.6 71.4 %all-gather.11.cloned.1.call-done = bf16[3584,1536]{1,0:T(8,128)(2,1)} async-done(((bf16[896,1536]{1,0:T(8,128)(2,1)}), bf16[3584,1536]{1,0:T(8,128)(2,1)}) %all-gather.11.cloned.1.call-update) | async-done | bytes 11010064 | tf_op jit(solution)/shard_map/all_gather | solution.py:70
  444.0 19.0 %add_convert_fusion = bf16[896,1536]{1,0:T(8,128)(2,1)} fusion(f32[896,1536]{1,0:T(8,128)} %get-tuple-element.6, bf16[896,3584]{0,1:T(8,128)(2,1)} %constant_dynamic-update-slice_fusion, s32[]{:T(128)S(6)} %select_n.38, bf16[3584,1536]{1,0:T(8,128)(2,1)} %all-gather.11.cloned.1.call-done, bf16[896,1536]{1,0:T(8,128)(2,1)} %get-tuple-element.3, f32[]{:T(128)S(6)} %sqrt.7), kind=kOutput, calls=%fused_computation.26 | convolution fusion | flops 9900785664 | bytes 28442632 | tf_op jit(solution)/shard_map/dot_general | solution.py:72
  463.1 73.2 %all-gather.13.cloned.1.call-done = bf16[3584,1536]{1,0:T(8,128)(2,1)} async-done(((bf16[896,1536]{1,0:T(8,128)(2,1)}), bf16[3584,1536]{1,0:T(8,128)(2,1)}) %all-gather.13.cloned.1.call-update) | async-done | bytes 11010064 | tf_op jit(solution)/shard_map/all_gather | solution.py:42
  536.4 13.1 %fusion.3 = bf16[3584,1536]{1,0:T(8,128)(2,1)S(1)} fusion(s32[]{:T(128)S(6)} %select_n.38, bf16[3584,1536]{1,0:T(8,128)(2,1)} %all-gather.13.cloned.1.call-done), kind=kLoop, calls=%fused_computation.13 | loop fusion | flops 22020096 | bytes 22020100 | tf_op jit(solution)/shard_map/jit(_roll_dynamic)/concatenate | solution.py:43
  549.4 4.2 copy-done
  553.6 10.3 %fusion.19 = bf16[896,2688]{0,1:T(8,128)(2,1)} fusion(bf16[896,1536]{1,0:T(8,128)(2,1)S(1)} %copy-done.2, bf16[3584,1536]{1,0:T(8,128)(2,1)S(1)} %fusion.3), kind=kOutput, calls=%fused_computation.29 | convolution fusion | flops 7401160704 | bytes 15826944 | tf_op jit(solution)/shard_map/dot_general | solution.py:26
  564.0 97.2 %reduce-scatter.5.cloned.1.call-done = bf16[896,336]{0,1:T(8,128)(2,1)} async-done(((bf16[896,2688]{0,1:T(8,128)(2,1)}), bf16[896,336]{0,1:T(8,128)(2,1)}) %reduce-scatter.5.cloned.1.call-update) | async-done | bytes 602128 | tf_op jit(solution)/shard_map/reduce_scatter | solution.py:46
  661.3 81.9 %all-gather.15.cloned.1.call-done = bf16[896,2688]{0,1:T(8,128)(2,1)} async-done(((bf16[896,336]{0,1:T(8,128)(2,1)}), bf16[896,2688]{0,1:T(8,128)(2,1)}) %all-gather.15.cloned.1.call-update) | async-done | bytes 4816912 | tf_op jit(solution)/shard_map/all_gather | solution.py:61
  746.6 2.7 constant_dynamic-update-slice_fusion.3
  749.4 17.4 %collective-permute-done.1 = bf16[896,896]{0,1:T(8,128)(2,1)S(1)} collective-permute-done((bf16[896,896]{0,1:T(8,128)(2,1)S(1)}, bf16[896,896]{0,1:T(8,128)(2,1)S(1)}, u32[]{:S(2)}, u32[]{:S(2)}) %collective-permute-start.1) | collective-permute-done | bytes 1605664 | tf_op jit(solution)/shard_map/ppermute | solution.py:22
  767.1 17.4 %fusion.38 = (bf16[896,1536]{1,0:T(8,128)(2,1)}, f32[896,1536]{1,0:T(8,128)}) fusion(bf16[896,3584]{0,1:T(8,128)(2,1)S(1)} %constant_dynamic-update-slice_fusion.2, bf16[3584,1536]{1,0:T(8,128)(2,1)} %copy-done), kind=kOutput, calls=%fused_computation.53 | convolution fusion | flops 9866379264 | bytes 25690112 | tf_op jit(solution)/shard_map/dot_general | solution.py:69
  784.5 71.7 %all-gather.17.cloned.1.call-done = bf16[3584,1536]{1,0:T(8,128)(2,1)} async-done(((bf16[896,1536]{1,0:T(8,128)(2,1)}), bf16[3584,1536]{1,0:T(8,128)(2,1)}) %all-gather.17.cloned.1.call-update) | async-done | bytes 11010064 | tf_op jit(solution)/shard_map/all_gather | solution.py:70
  856.2 18.7 %multiply_convert_fusion.1 = bf16[896,1536]{1,0:T(8,128)(2,1)} fusion(f32[896,1536]{1,0:T(8,128)} %get-tuple-element.8, bf16[896,1536]{1,0:T(8,128)(2,1)S(1)} %copy-done.3, bf16[896,3584]{0,1:T(8,128)(2,1)} %copy-done.1, s32[]{:T(128)S(6)} %select_n.38, bf16[3584,1536]{1,0:T(8,128)(2,1)} %all-gather.17.cloned.1.call-done), kind=kOutput, calls=%fused_computation.25 | convolution fusion | flops 9898033152 | bytes 28442628 | tf_op jit(solution)/shard_map/dot_general | solution.py:72
  (38 shorter events, 11.0 us)
Async XLA Ops:
  7.2 84.0 %all-gather.7.cloned.1.call-start = ((), (), s32[]{:S(2)}) async-start(), calls=%async_computation.2 | async-start | bytes 13762560 | tf_op jit(solution)/shard_map/all_gather | solution.py:42
  15.1 188.9 %reduce-scatter.3.cloned.1.call-start = ((), (), s32[]{:S(2)}) async-start(), calls=%async_computation.3 | async-start | bytes 5419008 | tf_op jit(solution)/shard_map/reduce_scatter | solution.py:46
  106.7 222.6 %all-gather.9.cloned.1.call-start = ((), (), s32[]{:S(2)}) async-start(), calls=%async_computation.4 | async-start | bytes 5419008 | tf_op jit(solution)/shard_map/all_gather | solution.py:61
  248.6 195.4 %all-gather.11.cloned.1.call-start = ((), (), s32[]{:S(2)}) async-start(), calls=%async_computation.5 | async-start | bytes 13762560 | tf_op jit(solution)/shard_map/all_gather | solution.py:70
  332.5 7.0 slice-start
  332.5 7.0 slice-start.1
  332.5 20.4 %collective-permute-start = (bf16[896,896]{0,1:T(8,128)(2,1)S(1)}, bf16[896,896]{0,1:T(8,128)(2,1)S(1)}, u32[]{:S(2)}, u32[]{:S(2)}) collective-permute-start(bf16[896,896]{0,1:T(8,128)(2,1)S(1)} %bitcast.11), channel_id=1, source_target_pairs={{0,8},{8,16},{16,24},{24,0},{1,9},{9,17},{17,25},{25,1},{2,10},{10... | collective-permute-start | bytes 4816904 | tf_op jit(solution)/shard_map/ppermute | solution.py:22
  372.4 164.0 %all-gather.13.cloned.1.call-start = ((), (), s32[]{:S(2)}) async-start(), calls=%async_computation.6 | async-start | bytes 13762560 | tf_op jit(solution)/shard_map/all_gather | solution.py:42
  463.1 90.6 %copy-start.2 = (bf16[896,1536]{1,0:T(8,128)(2,1)S(1)}, bf16[896,1536]{1,0:T(8,128)(2,1)}, u32[]{:S(2)}) copy-start(bf16[896,1536]{1,0:T(8,128)(2,1)} %add_convert_fusion) | copy-start | bytes 8257540
  463.1 198.1 %reduce-scatter.5.cloned.1.call-start = ((), (), s32[]{:S(2)}) async-start(), calls=%async_computation.7 | async-start | bytes 5419008 | tf_op jit(solution)/shard_map/reduce_scatter | solution.py:46
  549.4 4.2 copy-start
  564.0 179.2 %all-gather.15.cloned.1.call-start = ((), (), s32[]{:S(2)}) async-start(), calls=%async_computation.8 | async-start | bytes 5419008 | tf_op jit(solution)/shard_map/all_gather | solution.py:61
  661.2 195.0 %all-gather.17.cloned.1.call-start = ((), (), s32[]{:S(2)}) async-start(), calls=%async_computation.9 | async-start | bytes 13762560 | tf_op jit(solution)/shard_map/all_gather | solution.py:70
  746.3 20.5 %collective-permute-start.1 = (bf16[896,896]{0,1:T(8,128)(2,1)S(1)}, bf16[896,896]{0,1:T(8,128)(2,1)S(1)}, u32[]{:S(2)}, u32[]{:S(2)}) collective-permute-start(bf16[896,896]{0,1:T(8,128)(2,1)S(1)} %bitcast.12), channel_id=1, source_target_pairs={{0,8},{8,16},{16,24},{24,0},{1,9},{9,17},{17,25},{25,1},{2,10},{10... | collective-permute-start | bytes 4816904 | tf_op jit(solution)/shard_map/ppermute | solution.py:22
  767.1 17.5 %copy-start.1 = (bf16[896,3584]{0,1:T(8,128)(2,1)}, bf16[896,3584]{0,1:T(8,128)(2,1)S(1)}, u32[]{:S(2)}) copy-start(bf16[896,3584]{0,1:T(8,128)(2,1)S(1)} %constant_dynamic-update-slice_fusion.2) | copy-start | bytes 19267588
  767.1 89.1 %copy-start.3 = (bf16[896,1536]{1,0:T(8,128)(2,1)S(1)}, bf16[896,1536]{1,0:T(8,128)(2,1)}, u32[]{:S(2)}) copy-start(bf16[896,1536]{1,0:T(8,128)(2,1)} %add_convert_fusion) | copy-start | bytes 8257540
Sparse Core Ops, SparseCore 0:
  15.2 75.8 all-gather.6
  106.8 97.0 reduce-scatter.2
  248.8 80.5 all-gather.8
  372.5 71.4 all-gather.10
  463.2 73.1 all-gather.12
  564.1 97.0 reduce-scatter.4
  663.4 79.7 all-gather.14
  784.7 71.4 all-gather.16
where the time goes:
time: 889 us; the launch traced here: 882 us
  waiting for transfers between devices  678 us (76%)
  matrix products  99.1 us (11%)
  blocking collectives  39.7 us (4%)
  other arithmetic  31.8 us (4%)
  local copies, waits for them, and re-layouts  17.3 us (2%)
  between operations  15.5 us (2%)
    reduce_scatter x2, waiting for transfers between devices, per_device(): lax.psum_scatter(partial_value.astype(jnp.bfloat16), 'col', scatter_dimen...  194 us
    all_gather x2, waiting for transfers between devices, per_device(): lax.all_gather(shares.astype(jnp.bfloat16), 'col', axis=1, tiled=True)  163 us
    all_gather x2, waiting for transfers between devices, per_device(): panel = lax.all_gather(iterate, 'row', axis=0, tiled=True)  149 us
    all_gather x2, waiting for transfers between devices, per_device(): lax.all_gather(product.astype(jnp.bfloat16), 'row', axis=0, tiled=True)  143 us
    psum x1, blocking collectives, per_device(): quartic = lax.psum(jnp.sum(weights * shares * shares), ('row', 'col'))  39.7 us
    dot_general x2, matrix products, per_device(): second = jnp.dot(gram, product_panel, preferred_element_type=jnp.float32)  37.7 us
    dot_general x2, matrix products, per_device(): product = jnp.dot(gram, ordered, preferred_element_type=jnp.float32)  35.6 us
    ppermute x2, waiting for transfers between devices, passed_along(): lax.ppermute(shard, axis, [(i, (i + by) % count) for i in range(count)])  28.3 us
  transfers between devices with their start and end apart: 10, of which 10 were waited for; matrix products, arithmetic and copies ran while one was open for 1% of the time, Pallas kernels for 0%

commit v1 on v0

v1 whole, which is shorter than its diff:
```python
import functools
import math

import jax
import jax.numpy as jnp
from jax import lax
from jax.experimental import pallas as pl
from jax.experimental.pallas import tpu as pltpu
from jax.sharding import PartitionSpec as P

ITERS = 2

MOMENTUM_DECAY = 0.95
EPSILON = 1e-07
COEF_LINEAR = 3.4445
COEF_CUBIC = -4.775
COEF_QUINTIC = 2.0315


def outer_rows(left, right):
    return lax.dot_general(
        left, right, (((1,), (1,)), ((), ())), preferred_element_type=jnp.float32
    )


def chain_kernel(tile, factor, scale_ref, gram_ref, x_ref, out_ref, first, one, two, rough, exact, total):
    scale = scale_ref[0, 0]
    square = scale * scale
    size = gram_ref.shape[0]

    def times_gram(source, finish):
        @pl.loop(0, size // tile)
        def _(step):
            columns = pl.ds(pl.multiple_of(step * tile, tile), tile)
            value = jnp.dot(
                source[...], gram_ref[:, columns], preferred_element_type=jnp.float32
            )
            finish(columns, value * square)

    def polynomial(source, target):
        def keep(columns, value):
            exact[:, columns] = value
            rough[:, columns] = value.astype(jnp.bfloat16)

        def combine(columns, value):
            target[:, columns] = (
                COEF_LINEAR * source[:, columns].astype(jnp.float32)
                + COEF_CUBIC * exact[:, columns]
                + COEF_QUINTIC * value
            ).astype(jnp.bfloat16)

        times_gram(source, keep)
        times_gram(rough, combine)

    polynomial(x_ref, first)
    polynomial(first, one)
    polynomial(one, two)

    def after_product(columns, value):
        total[:, columns] = (
            COEF_LINEAR * first[:, columns].astype(jnp.float32) + COEF_CUBIC * value
        )
        one[:, columns] = value.astype(jnp.bfloat16)

    times_gram(two, after_product)
    polynomial(one, two)
    polynomial(two, one)

    def after_second(columns, value):
        out_ref[:, columns] = (
            (total[:, columns] + COEF_QUINTIC * value) * (scale * factor)
        ).astype(jnp.bfloat16)

    times_gram(one, after_second)


def chain(scale, gram, slab, factor):
    width, size = slab.shape
    tile = 512 if size % 512 == 0 else size
    vmem = pl.BlockSpec(memory_space=pltpu.VMEM)
    half = pltpu.VMEM((width, size), jnp.bfloat16)
    full = pltpu.VMEM((width, size), jnp.float32)
    return pl.pallas_call(
        functools.partial(chain_kernel, tile, factor),
        out_shape=jax.ShapeDtypeStruct((width, size), jnp.bfloat16),
        in_specs=[pl.BlockSpec(memory_space=pltpu.SMEM), vmem, vmem],
        out_specs=vmem,
        scratch_shapes=[half, half, half, half, full, full],
        compiler_params=pltpu.CompilerParams(vmem_limit_bytes=62 * 1024 * 1024),
        name="chain",
    )(scale.reshape(1, 1), gram, slab)


def assembled(shares, rows, block):
    half = block // 2
    middle = rows // 2

    def at(i, j):
        offset = (i - j) % rows
        if offset < middle:
            return shares[j, offset * block : (offset + 1) * block]
        if offset > middle:
            return at(j, i).T
        low, high = min(i, j), max(i, j)
        value = jnp.concatenate([shares[low, -half:], shares[high, -half:]], axis=0)
        return value if i == low else value.T

    return jnp.concatenate(
        [
            jnp.concatenate([at(i, j) for j in range(rows)], axis=1)
            for i in range(rows)
        ],
        axis=0,
    )


def per_device(factor, gradient, momentum):
    rows = lax.axis_size("row")
    grad32 = gradient.astype(jnp.float32)
    buffer = MOMENTUM_DECAY * momentum + grad32
    nesterov = grad32 + MOMENTUM_DECAY * buffer
    base = nesterov.astype(jnp.bfloat16)
    block = base.shape[0]
    half = block // 2
    middle = rows // 2
    me = lax.axis_index("row")
    panel = lax.all_gather(base, "row", axis=0, tiled=True)

    def rows_of(offset):
        start = ((me + offset) % rows) * block
        return lax.dynamic_slice_in_dim(panel, start, block, axis=0)

    parts = [outer_rows(base, base)]
    for offset in range(1, middle):
        parts.append(outer_rows(rows_of(offset), base))
    facing = rows_of(middle)
    lower = me < middle
    parts.append(
        outer_rows(
            jnp.where(lower, base[:half], facing[half:]), jnp.where(lower, facing, base)
        )
    )
    partial_value = jnp.concatenate([part.astype(jnp.bfloat16) for part in parts], axis=0)
    share = lax.psum_scatter(partial_value, "col", scatter_dimension=0, tiled=True)
    shares = lax.all_gather(share, ("row", "col"), axis=0, tiled=True)
    shares = shares.reshape(rows, -1, block)
    gram = assembled(shares, rows, block)
    quartic = jnp.sum(jnp.square(gram.astype(jnp.float32)))
    scale = 1.0 / jnp.sqrt(jnp.sqrt(quartic) + EPSILON)

    width = panel.shape[1] // rows
    slab = lax.dynamic_slice_in_dim(panel, me * width, width, axis=1).T
    update = chain(scale, gram, slab, factor).T
    update = lax.all_to_all(update, "row", 0, 1, tiled=True)
    return (update, buffer)


def solution(mesh):
    def whole(gradient, momentum):
        factor = 0.2 * math.sqrt(max(gradient.shape))
        return jax.shard_map(
            functools.partial(per_device, factor),
            mesh=mesh,
            in_specs=(P("row", "col"), P("row", "col")),
            out_specs=(P("row", "col"), P("row", "col")),
            check_vma=False,
        )(gradient, momentum)

    return whole
```

time: 889 us -> 701 us (0.79)
  waiting for transfers between devices: 678 us -> 308 us
  Pallas kernels: 0 us -> 145 us
  other arithmetic: 31.8 us -> 123 us
  matrix products: 99.1 us -> 16.2 us
  local copies, waits for them, and re-layouts: 17.3 us -> 79.3 us
  blocking collectives: 39.7 us -> 0 us
    all_gather x6 -> x2, waiting for transfers between devices: 455 us -> 179 us  [the longest x1 110 us: per_device(): shares = lax.all_gather(share, ('row', 'col'), axis=0, tiled=True)]
    reduce_scatter x2 -> x0, waiting for transfers between devices: 194 us -> none  [per_device(): lax.psum_scatter(partial_value.astype(jnp.bfloat16), 'col', scatter_dimen...]
    pallas_call x0 -> x1, Pallas kernels: none -> 145 us  [chain(): pl.pallas_call(functools.partial(chain_kernel, tile, factor), out_shape=j...]
    unnamed x8 -> x4, waiting for transfers between devices: 0.13 us -> 103 us
    dot_general x4 -> x0, matrix products: 73.3 us -> none  [the longest x2 37.7 us: per_device(): second = jnp.dot(gram, product_panel, preferred_element_type=jnp.float32)]
    reduce_sum x1, other arithmetic: 2.16 us -> 69.7 us  [per_device(): quartic = jnp.sum(jnp.square(gram.astype(jnp.float32)))]
    psum x1 -> x0, blocking collectives: 39.7 us -> none  [per_device(): quartic = lax.psum(jnp.sum(weights * shares * shares), ('row', 'col'))]
    ppermute x2 -> x0, waiting for transfers between devices: 28.3 us -> none  [passed_along(): lax.ppermute(shard, axis, [(i, (i + by) % count) for i in range(count)])]
  transfers between devices with their start and end apart: 10 -> 4, of which waited for: 10 -> 4; matrix products, arithmetic and copies ran while one was open for 1% -> 2% of each run, Pallas kernels for 0% -> 0%
where the time goes in v1:
time: 701 us; the launch traced here: 691 us
  waiting for transfers between devices  308 us (44%)
  Pallas kernels  145 us (21%)
  other arithmetic  123 us (18%)
  local copies, waits for them, and re-layouts  79.3 us (11%)
  matrix products  16.2 us (2%)
  between operations  15 us (2%)
    pallas_call x1, Pallas kernels, chain(): pl.pallas_call(functools.partial(chain_kernel, tile, factor), out_shape=j...  145 us
    all_gather x1, waiting for transfers between devices, per_device(): shares = lax.all_gather(share, ('row', 'col'), axis=0, tiled=True)  110 us
    unnamed x4, waiting for transfers between devices  103 us
    reduce_sum x1, other arithmetic, per_device(): quartic = jnp.sum(jnp.square(gram.astype(jnp.float32)))  69.7 us
    all_gather x1, waiting for transfers between devices, per_device(): panel = lax.all_gather(base, 'row', axis=0, tiled=True)  68.9 us
    unnamed x14, local copies, waits for them, and re-layouts  33.1 us
    concatenate x2, other arithmetic, assembled(): jnp.concatenate([at(i, j) for j in range(rows)], axis=1)  31.3 us
    all_to_all x1, waiting for transfers between devices, per_device(): update = lax.all_to_all(update, 'row', 0, 1, tiled=True)  26.6 us
  transfers between devices with their start and end apart: 4, of which 4 were waited for; matrix products, arithmetic and copies ran while one was open for 2% of the time, Pallas kernels for 0%

profile of v1, /device:TPU:0, one launch (start us, length us, event | category | flops | bytes accessed | tf_op | source)
XLA Modules:
  0.0 690.8 jit_solution(17128071515607947258)
XLA Ops:
  10.5 6.1 copy.19
  16.6 6.9 %convert_add_fusion.1 = (f32[896,1536]{0,1:T(8,128)}, bf16[896,1536]{0,1:T(8,128)(2,1)}) fusion(bf16[896,1536]{0,1:T(8,128)(2,1)S(1)} %copy.18, f32[896,1536]{0,1:T(8,128)} %copy.19), kind=kLoop, calls=%fused_computation.3 | loop fusion | flops 8257536 | bytes 16515072 | tf_op jit(solution)/shard_map/add | solution.py:120
  23.7 7.0 %convolution_convert_fusion = bf16[896,896]{1,0:T(8,128)(2,1)} fusion(bf16[896,1536]{0,1:T(8,128)(2,1)} %get-tuple-element.23), kind=kOutput, calls=%fused_computation.16 | convolution fusion | flops 2467053568 | bytes 4358144 | tf_op jit(solution)/shard_map/dot_general | solution.py:21
  30.6 68.9 %all-gather.3.cloned.1.call-done = bf16[3584,1536]{0,1:T(8,128)(2,1)} async-done(((bf16[896,1536]{0,1:T(8,128)(2,1)}), bf16[3584,1536]{0,1:T(8,128)(2,1)}) %all-gather.3.cloned.1.call-update) | async-done | bytes 11010064 | tf_op jit(solution)/shard_map/all_gather | solution.py:127
  99.5 4.8 fusion.7
  104.4 4.4 fusion.12
  108.8 8.8 %pad_maximum_fusion.2 = bf16[2240,896]{1,0:T(8,128)(2,1)} fusion(bf16[448,896]{1,0:T(8,128)(2,1)S(1)} %fusion.12, bf16[896,896]{1,0:T(8,128)(2,1)S(1)} %fusion.7, bf16[896,896]{1,0:T(8,128)(2,1)S(1)} %copy-done.1), kind=kLoop, calls=%fused_computation.7 | loop fusion | flops 12042240 | bytes 8028160 | tf_op jit(solution)/shard_map/concatenate | solution.py:143
  117.9 103.2 %reduce-scatter.4.cloned.1.call-done = bf16[280,896]{1,0:T(8,128)(2,1)} async-done(((bf16[2240,896]{1,0:T(8,128)(2,1)}), bf16[280,896]{1,0:T(8,128)(2,1)}) %reduce-scatter.4.cloned.1.call-update) | async-done | bytes 501776
  224.6 109.7 %all-gather.5.cloned.1.call-done = bf16[8960,896]{1,0:T(8,128)(2,1)} async-done(((bf16[280,896]{1,0:T(8,128)(2,1)}), bf16[8960,896]{1,0:T(8,128)(2,1)}) %all-gather.5.cloned.1.call-update) | async-done | bytes 16056336 | tf_op jit(solution)/shard_map/all_gather | solution.py:145
  334.4 3.6 fusion.18
  337.9 9.5 %fusion.17 = (bf16[1,896,896]{2,1,0:T(8,128)(2,1)S(1)}, bf16[896,896]{0,1:T(8,128)(2,1)}, bf16[896,896]{0,1:T(8,128)(2,1)}, bf16[1,896,896]{2,1,0:T(8,128)(2,1)S...) fusion(bf16[4,2240,896]{2,1,0:T(8,128)(2,1)} %bitcast.49), kind=kLoop, calls=%fused_computation.34 | loop fusion | bytes 28901376 | tf_op jit(solution)/shard_map/slice | solution.py:101
  362.0 3.6 copy.26
  365.5 17.1 %pad_maximum_fusion = bf16[896,3584]{0,1:T(8,128)(2,1)} fusion(bf16[896,896]{0,1:T(8,128)(2,1)S(1)} %bitcast.52, bf16[448,896]{0,1:T(8,128)(2,1)} %bitcast.60, bf16[448,896]{0,1:T(8,128)(2,1)} %bitcast.58, bf16[896,896]{0,1:T(8,128)(2,1)} %get-tuple-element.9, bf16[896,896]{0,1:T(8,128)(2,1)} %bitcast.61), kind=kLoop, calls=%fused_computation.4 | loop fusion | flops 32112640 | bytes 12845056 | tf_op jit(solution)/shard_map/concatenate | solution.py:110
  382.6 9.5 %copy.28 = bf16[896,3584]{1,0:T(8,128)(2,1)} copy(bf16[896,3584]{0,1:T(8,128)(2,1)} %pad_maximum_fusion) | data formatting | bytes 12845056 | tf_op jit(solution)/shard_map/concatenate | solution.py:110
  392.1 3.6 copy.38
  395.7 14.2 %pad_maximum_fusion.1 = bf16[896,3584]{0,1:T(8,128)(2,1)} fusion(bf16[896,896]{0,1:T(8,128)(2,1)} %get-tuple-element.10, bf16[896,896]{0,1:T(8,128)(2,1)} %bitcast.62, bf16[896,896]{0,1:T(8,128)(2,1)S(1)} %bitcast.50, bf16[896,896]{0,1:T(8,128)(2,1)} %copy.26), kind=kLoop, calls=%fused_computation.5 | loop fusion | flops 25690112 | bytes 12845056 | tf_op jit(solution)/shard_map/concatenate | solution.py:110
  409.9 9.5 %copy.29 = bf16[896,3584]{1,0:T(8,128)(2,1)} copy(bf16[896,3584]{0,1:T(8,128)(2,1)} %pad_maximum_fusion.1) | data formatting | bytes 12845056 | tf_op jit(solution)/shard_map/concatenate | solution.py:110
  422.1 3.6 copy.27
  425.6 69.7 %multiply_reduce_fusion = (f32[]{:T(128)}, bf16[3584,3584]{1,0:T(8,128)(2,1)}) fusion(bf16[896,896]{1,0:T(8,128)(2,1)} %get-tuple-element.15, bf16[896,896]{1,0:T(8,128)(2,1)} %get-tuple-element.14, bf16[896,896]{1,0:T(8,128)(2,1)} %copy.27, bf16[896,896]{1,0:T(8,128)(2,1)S(1)} %bitcast.53, bf16[896,3584]{1,0:T(8,128)(2,1)} %copy.29, ...), kind=kLoop, calls=%fused_computation | loop fusion | flops 321126400 | bytes 51380228 | tf_op jit(solution)/shard_map/reduce_sum | solution.py:148
  496.0 145.2 %chain.1 = bf16[384,3584]{1,0:T(8,128)(2,1)} custom-call(f32[1,1]{1,0:T(1,128)} %bitcast.19.scale_ref, bf16[3584,3584]{1,0:T(8,128)(2,1)} %get-tuple-element.7.gram_ref, bf16[384,3584]{1,0:T(8,128)(2,1)} %dynamic-slice_bitcast_fusion.x_ref), custom_call_target="tpu_custom_call" | custom-call | tf_op jit(solution)/shard_map/chain/pallas_call | solution.py:83
  641.3 3.5 copy.41
  644.8 3.7 all-to-all-start
  648.5 6.1 copy.32
  654.6 26.6 %all-to-all-done = bf16[4,896,384]{1,2,0:T(8,128)(2,1)S(1)} async-done(((bf16[4,896,384]{1,2,0:T(8,128)(2,1)}), bf16[4,896,384]{1,2,0:T(8,128)(2,1)S(1)}, u32[]{:S(2)}, u32[]{:S(2)}) %all-to-all-start) | async-done | bytes 2752544 | tf_op jit(solution)/shard_map/all_to_all | solution.py:154
  (20 shorter events, 27.0 us)
Async XLA Ops:
  7.2 92.4 %all-gather.3.cloned.1.call-start = ((), (), s32[]{:S(2)}) async-start(), calls=%async_computation.2 | async-start | bytes 13762560 | tf_op jit(solution)/shard_map/all_gather | solution.py:127
  23.6 197.5 %reduce-scatter.4.cloned.1.call-start = ((), (), s32[]{:S(2)}) async-start(), calls=%async_computation.4 | async-start | bytes 4515840
  23.6 75.9 %copy-start = (bf16[896,1536]{0,1:T(8,128)(2,1)S(1)}, bf16[896,1536]{0,1:T(8,128)(2,1)}, u32[]{:S(2)}) copy-start(bf16[896,1536]{0,1:T(8,128)(2,1)} %get-tuple-element.23) | copy-start | bytes 8257540
  104.4 4.5 copy-start.1
  117.7 216.7 %all-gather.5.cloned.1.call-start = ((), (), s32[]{:S(2)}) async-start(), calls=%async_computation.3 | async-start | bytes 16558080 | tf_op jit(solution)/shard_map/all_gather | solution.py:145
  644.8 36.3 %all-to-all-start = ((bf16[4,896,384]{1,2,0:T(8,128)(2,1)}), bf16[4,896,384]{1,2,0:T(8,128)(2,1)S(1)}, u32[]{:S(2)}, u32[]{:S(2)}) async-start(bf16[4,896,384]{1,2,0:T(8,128)(2,1)} %bitcast.55), calls=%async_computation | async-start | bytes 5505024 | tf_op jit(solution)/shard_map/all_to_all | solution.py:154
Sparse Core Ops, SparseCore 0:
  23.7 75.7 all-gather.2
  117.8 103.2 reduce-scatter.3
  224.1 110.2 all-gather.4

commit v2 on v1

--- a/solution.py
+++ b/solution.py
@@ -23,10 +23,67 @@
     )
 
 
-def chain_kernel(tile, factor, scale_ref, gram_ref, x_ref, out_ref, first, one, two, rough, exact, total):
-    scale = scale_ref[0, 0]
+def direct_blocks(rows, block):
+    if rows == 1:
+        return [(0, 0, block, 0, 0)]
+    half = block // 2
+    middle = rows // 2
+    found = []
+    for j in range(rows):
+        for offset in range(middle):
+            i = (j + offset) % rows
+            found.append((j, offset * block, block, i * block, j * block))
+        low, high = min(j, (j + middle) % rows), max(j, (j + middle) % rows)
+        top = low * block + (0 if j == low else half)
+        found.append((j, middle * block, half, top, high * block))
+    return found
+
+
+def mirrored_blocks(rows):
+    if rows == 1:
+        return []
+    middle = rows // 2
+    pairs = [((j + k) % rows, j) for j in range(rows) for k in range(1, middle)]
+    return pairs + [(low, low + middle) for low in range(middle)]
+
+
+def chain_kernel(
+    tile, factor, rows, shares_ref, x_ref, out_ref, gram_ref, first, one, two, rough, exact, total, sems
+):
+    size = gram_ref.shape[0]
+    block = size // rows
+    stride = shares_ref.shape[0] // rows
+    strip = 128
+    copies = []
+    for number, (owner, start, height, row, column) in enumerate(direct_blocks(rows, block)):
+        copies.append(
+            pltpu.make_async_copy(
+                shares_ref.at[pl.ds(owner * stride + start, height), :],
+                gram_ref.at[pl.ds(row, height), pl.ds(column, block)],
+                sems.at[number],
+            )
+        )
+    for copy in copies:
+        copy.start()
+    for copy in copies:
+        copy.wait()
+
+    def squares(i, j, mirror):
+        def body(step, carry):
+            lanes = pl.ds(pl.multiple_of(j * block + step * strip, strip), strip)
+            piece = gram_ref[pl.ds(i * block, block), lanes]
+            if mirror:
+                gram_ref[lanes, pl.ds(i * block, block)] = piece.T
+            wide = piece.astype(jnp.float32)
+            return carry + jnp.sum(wide * wide, axis=0, keepdims=True)
+
+        return lax.fori_loop(0, block // strip, body, jnp.zeros((1, strip), jnp.float32))
+
+    diagonal = sum(squares(i, i, False) for i in range(rows))
+    others = sum(squares(i, j, True) for i, j in mirrored_blocks(rows)) + jnp.zeros_like(diagonal)
+    quartic = jnp.sum(diagonal + 2.0 * others, axis=1, keepdims=True)
+    scale = 1.0 / jnp.sqrt(jnp.sqrt(quartic) + EPSILON)
     square = scale * scale
-    size = gram_ref.shape[0]
 
     def times_gram(source, finish):
         @pl.loop(0, size // tile)
@@ -52,7 +109,16 @@
         times_gram(source, keep)
         times_gram(rough, combine)
 
-    polynomial(x_ref, first)
+    width = x_ref.shape[1]
+    lanes_step = 128 if width % 128 == 0 else width
+
+    @pl.loop(0, size // strip)
+    def _(step):
+        chunk = pl.ds(pl.multiple_of(step * strip, strip), strip)
+        for lane in range(0, width, lanes_step):
+            two[lane : lane + lanes_step, chunk] = x_ref[chunk, lane : lane + lanes_step].T
+
+    polynomial(two, first)
     polynomial(first, one)
     polynomial(one, two)
 
@@ -67,28 +133,36 @@
     polynomial(two, one)
 
     def after_second(columns, value):
-        out_ref[:, columns] = (
+        two[:, columns] = (
             (total[:, columns] + COEF_QUINTIC * value) * (scale * factor)
         ).astype(jnp.bfloat16)
 
     times_gram(one, after_second)
 
-
-def chain(scale, gram, slab, factor):
-    width, size = slab.shape
+    @pl.loop(0, size // strip)
+    def _(step):
+        chunk = pl.ds(pl.multiple_of(step * strip, strip), strip)
+        for lane in range(0, width, lanes_step):
+            out_ref[chunk, lane : lane + lanes_step] = two[lane : lane + lanes_step, chunk].T
+
+
+def chain(shares, slab, factor, rows):
+    size, width = slab.shape
     tile = 512 if size % 512 == 0 else size
     vmem = pl.BlockSpec(memory_space=pltpu.VMEM)
     half = pltpu.VMEM((width, size), jnp.bfloat16)
     full = pltpu.VMEM((width, size), jnp.float32)
+    count = rows * (rows // 2 + 1)
     return pl.pallas_call(
-        functools.partial(chain_kernel, tile, factor),
-        out_shape=jax.ShapeDtypeStruct((width, size), jnp.bfloat16),
-        in_specs=[pl.BlockSpec(memory_space=pltpu.SMEM), vmem, vmem],
+        functools.partial(chain_kernel, tile, factor, rows),
+        out_shape=jax.ShapeDtypeStruct((size, width), jnp.bfloat16),
+        in_specs=[pl.BlockSpec(memory_space=pl.ANY), vmem],
         out_specs=vmem,
-        scratch_shapes=[half, half, half, half, full, full],
-        compiler_params=pltpu.CompilerParams(vmem_limit_bytes=62 * 1024 * 1024),
+        scratch_shapes=[pltpu.VMEM((size, size), jnp.bfloat16)]
+        + [half, half, half, half, full, full, pltpu.SemaphoreType.DMA((count,))],
+        compiler_params=pltpu.CompilerParams(vmem_limit_bytes=63 * 1024 * 1024),
         name="chain",
-    )(scale.reshape(1, 1), gram, slab)
+    )(shares, slab)
 
 
 def assembled(shares, rows, block):
@@ -143,14 +217,14 @@
     partial_value = jnp.concatenate([part.astype(jnp.bfloat16) for part in parts], axis=0)
     share = lax.psum_scatter(partial_value, "col", scatter_dimension=0, tiled=True)
     shares = lax.all_gather(share, ("row", "col"), axis=0, tiled=True)
-    shares = shares.reshape(rows, -1, block)
-    gram = assembled(shares, rows, block)
-    quartic = jnp.sum(jnp.square(gram.astype(jnp.float32)))
-    scale = 1.0 / jnp.sqrt(jnp.sqrt(quartic) + EPSILON)
+    parts = rows
+    if block % 128:
+        shares = assembled(shares.reshape(rows, -1, block), rows, block)
+        parts = 1
 
     width = panel.shape[1] // rows
-    slab = lax.dynamic_slice_in_dim(panel, me * width, width, axis=1).T
-    update = chain(scale, gram, slab, factor).T
+    slab = lax.dynamic_slice_in_dim(panel, me * width, width, axis=1)
+    update = chain(shares, slab, factor, parts)
     update = lax.all_to_all(update, "row", 0, 1, tiled=True)
     return (update, buffer)
 

time: 701 us -> 527 us (0.75); the launches traced: 691 us -> 527 us
  other arithmetic: 123 us -> 16.7 us
  local copies, waits for them, and re-layouts: 79.3 us -> 7.1 us
  blocking collectives: 0 us -> 36.3 us
  waiting for transfers between devices: 308 us -> 282 us
  Pallas kernels: 145 us -> 157 us
    reduce_sum x1 -> x0, other arithmetic: 69.7 us -> none  [per_device(): quartic = jnp.sum(jnp.square(gram.astype(jnp.float32)))]
    all_to_all x0 -> x1, blocking collectives: none -> 36.3 us  [per_device(): update = lax.all_to_all(update, 'row', 0, 1, tiled=True)]
    unnamed x14 -> x4, local copies, waits for them, and re-layouts: 33.1 us -> 1.67 us
    concatenate x2 -> x0, other arithmetic: 31.3 us -> none  [assembled(): jnp.concatenate([at(i, j) for j in range(rows)], axis=1)]
    all_to_all x1 -> x0, waiting for transfers between devices: 26.6 us -> none  [per_device(): update = lax.all_to_all(update, 'row', 0, 1, tiled=True)]
    concatenate x2 -> x0, local copies, waits for them, and re-layouts: 19 us -> none  [assembled(): jnp.concatenate([at(i, j) for j in range(rows)], axis=1)]
    slice x2 -> x0, local copies, waits for them, and re-layouts: 13.1 us -> none  [the longest x1 9.47 us: at(): return shares[j, offset * block:(offset + 1) * block]]
    pallas_call x1, Pallas kernels: 145 us -> 157 us  [chain(): pl.pallas_call(functools.partial(chain_kernel, tile, factor, rows), out_s...]
  transfers between devices with their start and end apart: 4 -> 3, of which waited for: 4 -> 3; matrix products, arithmetic and copies ran while one was open for 2% -> 1% of each run, Pallas kernels for 0% -> 0%
where the time goes in v2:
time: 527 us
  waiting for transfers between devices  282 us (54%)
  Pallas kernels  157 us (30%)
  blocking collectives  36.3 us (7%)
  other arithmetic  16.7 us (3%)
  between operations  13.8 us (3%)
  matrix products  12.9 us (2%)
  local copies, waits for them, and re-layouts  7.1 us (1%)
    pallas_call x1, Pallas kernels, chain(): pl.pallas_call(functools.partial(chain_kernel, tile, factor, rows), out_s...  157 us
    all_gather x1, waiting for transfers between devices, per_device(): shares = lax.all_gather(share, ('row', 'col'), axis=0, tiled=True)  110 us
    unnamed x4, waiting for transfers between devices  103 us
    all_gather x1, waiting for transfers between devices, per_device(): panel = lax.all_gather(base, 'row', axis=0, tiled=True)  70.1 us
    all_to_all x1, blocking collectives, per_device(): update = lax.all_to_all(update, 'row', 0, 1, tiled=True)  36.3 us
    dot_general x3, matrix products, outer_rows(): lax.dot_general(left, right, (((1,), (1,)), ((), ())), preferred_element_...  12.9 us
  transfers between devices with their start and end apart: 3, of which 3 were waited for; matrix products, arithmetic and copies ran while one was open for 1% of the time, Pallas kernels for 0%

profile of v2, /device:TPU:0, one launch (start us, length us, event | category | flops | bytes accessed | tf_op | source)
XLA Modules:
  0.0 526.9 jit_solution(14998610838996761819)
XLA Ops:
  7.2 0.0 all-gather.3.cloned.1.call-start
  7.2 7.9 %fusion = (bf16[896,1536]{1,0:T(8,128)(2,1)}, f32[896,1536]{1,0:T(8,128)}) fusion(bf16[896,1536]{1,0:T(8,128)(2,1)} %param.2, f32[896,1536]{1,0:T(8,128)} %param.3), kind=kLoop, calls=%fused_computation.2 | loop fusion | flops 8257536 | bytes 16515072 | tf_op jit(solution)/shard_map/convert_element_type | solution.py:196
  15.1 0.0 copy-start
  15.1 0.0 all-gather.3.cloned.1.call-update
  15.1 0.0 reduce-scatter.4.cloned.1.call-start
  15.2 1.7 copy-done
  16.9 4.2 convolution_convert_fusion
  21.0 70.1 %all-gather.3.cloned.1.call-done = bf16[3584,1536]{1,0:T(8,128)(2,1)} async-done(((bf16[896,1536]{1,0:T(8,128)(2,1)}), bf16[3584,1536]{1,0:T(8,128)(2,1)}) %all-gather.3.cloned.1.call-update) | async-done | bytes 11010064 | tf_op jit(solution)/shard_map/all_gather | solution.py:201
  91.2 4.8 fusion.7
  96.0 0.0 copy-start.1
  96.0 3.9 fusion.10
  99.9 0.0 copy-done.1
  99.9 8.8 %pad_maximum_fusion = bf16[2240,896]{1,0:T(8,128)(2,1)} fusion(bf16[448,896]{1,0:T(8,128)(2,1)S(1)} %fusion.10, bf16[896,896]{1,0:T(8,128)(2,1)S(1)} %fusion.7, bf16[896,896]{1,0:T(8,128)(2,1)S(1)} %copy-done.1), kind=kLoop, calls=%fused_computation.3 | loop fusion | flops 12042240 | bytes 8028160 | tf_op jit(solution)/shard_map/concatenate | solution.py:217
  108.7 0.0 reduce-scatter.4.cloned.1.call-update
  108.8 0.2 all-gather.5.cloned.1.call-start
  109.0 102.6 %reduce-scatter.4.cloned.1.call-done = bf16[280,896]{1,0:T(8,128)(2,1)} async-done(((bf16[2240,896]{1,0:T(8,128)(2,1)}), bf16[280,896]{1,0:T(8,128)(2,1)}) %reduce-scatter.4.cloned.1.call-update) | async-done | bytes 501776
  211.6 0.0 all-gather.5.cloned.1.call-update
  211.6 3.6 constant_dynamic-slice_fusion.x_ref
  215.2 109.6 %all-gather.5.cloned.1.call-done.shares_ref = bf16[8960,896]{1,0:T(8,128)(2,1)} async-done(((bf16[280,896]{1,0:T(8,128)(2,1)}), bf16[8960,896]{1,0:T(8,128)(2,1)}) %all-gather.5.cloned.1.call-update) | async-done | bytes 16056336 | tf_op jit(solution)/shard_map/all_gather | solution.py:219
  324.9 157.3 %chain.1 = bf16[3584,384]{1,0:T(8,128)(2,1)} custom-call(bf16[8960,896]{1,0:T(8,128)(2,1)} %all-gather.5.cloned.1.call-done.shares_ref, bf16[3584,384]{1,0:T(8,128)(2,1)} %constant_dynamic-slice_fusion.x_ref), custom_call_target="tpu_custom_call" | custom-call | tf_op jit(solution)/shard_map/chain/pallas_call | solution.py:156
  482.2 36.3 %all_to_all.19 = bf16[4,896,384]{2,1,0:T(8,128)(2,1)S(1)} all-to-all(bf16[4,896,384]{2,1,0:T(8,128)(2,1)} %bitcast.9), channel_id=1, replica_groups=mesh['row'=4,'col'=8] {'row'}, dimensions={0} | all-to-all | bytes 5505024 | tf_op jit(solution)/shard_map/all_to_all | solution.py:228
  518.5 1.8 copy.6
Async XLA Ops:
  7.2 84.0 %all-gather.3.cloned.1.call-start = ((), (), s32[]{:S(2)}) async-start(), calls=%async_computation.2 | async-start | bytes 13762560 | tf_op jit(solution)/shard_map/all_gather | solution.py:201
  15.1 1.8 copy-start
  15.1 196.5 %reduce-scatter.4.cloned.1.call-start = ((), (), s32[]{:S(2)}) async-start(), calls=%async_computation.4 | async-start | bytes 4515840
  96.0 4.0 copy-start.1
  108.8 216.1 %all-gather.5.cloned.1.call-start = ((), (), s32[]{:S(2)}) async-start(), calls=%async_computation.3 | async-start | bytes 16558080 | tf_op jit(solution)/shard_map/all_gather | solution.py:219
Sparse Core Ops, SparseCore 0:
  15.2 75.8 all-gather.2
  108.9 102.6 reduce-scatter.3
  214.6 110.2 all-gather.4

commit v3 on v2

--- a/solution.py
+++ b/solution.py
@@ -188,6 +188,86 @@
     )
 
 
+def ring_kernel(partial_ref, out_ref, *scratch):
+    landed, running, send_sems, recv_sems = scratch[:2], scratch[2:4], scratch[4], scratch[5]
+    count = partial_ref.shape[0]
+    column = lax.axis_index("col")
+    odd, pair = lax.rem(column, 2), lax.div(column, 2)
+    place = (1 - odd) * pair + odd * (count - 1 - pair)
+    sign = 1 - 2 * lax.rem(lax.axis_index("row"), 2)
+    ways = (sign, -sign)
+    wide = landed[0].shape[2]
+    lanes = (pl.ds(0, wide), pl.ds(wide, landed[1].shape[2]))
+
+    def column_at(spot):
+        spot = lax.rem(spot + 2 * count, count)
+        back = lax.div(spot, count // 2)
+        return (1 - back) * 2 * spot + back * (2 * (count - 1 - spot) + 1)
+
+    barrier = pltpu.get_barrier_semaphore()
+    for way in ways:
+        pl.semaphore_signal(
+            barrier,
+            inc=1,
+            device_id={"col": column_at(place + way)},
+            device_id_type=pl.DeviceIdType.MESH,
+        )
+    pl.semaphore_wait(barrier, 2)
+
+    def copy_of(step, k, source):
+        return pltpu.make_async_remote_copy(
+            src_ref=source,
+            dst_ref=landed[k].at[step],
+            send_sem=send_sems.at[k, step],
+            recv_sem=recv_sems.at[k, step],
+            device_id={"col": column_at(place + ways[k])},
+            device_id_type=pl.DeviceIdType.MESH,
+        )
+
+    copies = []
+    for k in range(2):
+        source = partial_ref.at[column_at(place - ways[k]), :, lanes[k]]
+        copies.append([copy_of(0, k, source)])
+        copies[k][0].start()
+    for step in range(count - 1):
+        for k in range(2):
+            copies[k][step].wait_recv()
+            mine = partial_ref[column_at(place - ways[k] * (step + 2)), :, lanes[k]]
+            value = landed[k][step].astype(jnp.float32) + mine.astype(jnp.float32)
+            value = value.astype(jnp.bfloat16)
+            if step < count - 2:
+                running[k][step] = value
+                copies[k].append(copy_of(step + 1, k, running[k].at[step]))
+                copies[k][step + 1].start()
+            else:
+                out_ref[:, lanes[k]] = value
+    for k in range(2):
+        for copy in copies[k]:
+            copy.wait_send()
+
+
+def ring_sum(partial_value, count):
+    block = partial_value.shape[1]
+    height = partial_value.shape[0] // count
+    wide = (block // 128 + 1) // 2 * 128
+    vmem = pl.BlockSpec(memory_space=pltpu.VMEM)
+    slots = [
+        pltpu.VMEM((count - 1, height, width), jnp.bfloat16) for width in (wide, block - wide)
+    ]
+    sems = pltpu.SemaphoreType.DMA((2, count - 1))
+    return pl.pallas_call(
+        ring_kernel,
+        out_shape=jax.ShapeDtypeStruct((height, block), jnp.bfloat16),
+        in_specs=[vmem],
+        out_specs=vmem,
+        scratch_shapes=slots + slots + [sems, sems],
+        compiler_params=pltpu.CompilerParams(
+            collective_id=0, has_side_effects=True, vmem_limit_bytes=40 * 1024 * 1024
+        ),
+        name="ring_sum",
+    )(partial_value.reshape(count, height, block))
+
+
 def per_device(factor, gradient, momentum):
     rows = lax.axis_size("row")
     grad32 = gradient.astype(jnp.float32)
@@ -215,7 +295,11 @@
         )
     )
     partial_value = jnp.concatenate([part.astype(jnp.bfloat16) for part in parts], axis=0)
-    share = lax.psum_scatter(partial_value, "col", scatter_dimension=0, tiled=True)
+    count = lax.axis_size("col")
+    if block % 128 or count % 2 or count < 4:
+        share = lax.psum_scatter(partial_value, "col", scatter_dimension=0, tiled=True)
+    else:
+        share = ring_sum(partial_value, count)
     shares = lax.all_gather(share, ("row", "col"), axis=0, tiled=True)
     parts = rows
     if block % 128:

time: 527 us -> 474 us (0.90)
  waiting for transfers between devices: 282 us -> 175 us
  Pallas kernels: 157 us -> 213 us
    unnamed x4 -> x2, waiting for transfers between devices: 103 us -> 0.03 us
    pallas_call x0 -> x1, Pallas kernels: none -> 55.3 us  [ring_sum(): pl.pallas_call(ring_kernel, out_shape=jax.ShapeDtypeStruct((height, block...]
  transfers between devices with their start and end apart: 3 -> 2, of which waited for: 3 -> 2; matrix products, arithmetic and copies ran while one was open for 1% -> 2% of each run, Pallas kernels for 0% -> 0%
where the time goes in v3:
time: 474 us
  Pallas kernels  213 us (45%)
  waiting for transfers between devices  175 us (37%)
  blocking collectives  36.3 us (8%)
  other arithmetic  15.4 us (3%)
  between operations  14.1 us (3%)
  matrix products  12.9 us (3%)
  local copies, waits for them, and re-layouts  7.1 us (1%)
    pallas_call x1, Pallas kernels, chain(): pl.pallas_call(functools.partial(chain_kernel, tile, factor, rows), out_s...  157 us
    all_gather x1, waiting for transfers between devices, per_device(): shares = lax.all_gather(share, ('row', 'col'), axis=0, tiled=True)  105 us
    all_gather x1, waiting for transfers between devices, per_device(): panel = lax.all_gather(base, 'row', axis=0, tiled=True)  70.1 us
    pallas_call x1, Pallas kernels, ring_sum(): pl.pallas_call(ring_kernel, out_shape=jax.ShapeDtypeStruct((height, block...  55.3 us
    all_to_all x1, blocking collectives, per_device(): update = lax.all_to_all(update, 'row', 0, 1, tiled=True)  36.3 us
    dot_general x3, matrix products, outer_rows(): lax.dot_general(left, right, (((1,), (1,)), ((), ())), preferred_element_...  12.9 us
  transfers between devices with their start and end apart: 2, of which 2 were waited for; matrix products, arithmetic and copies ran while one was open for 2% of the time, Pallas kernels for 0%

profile of v3, /device:TPU:0, one launch (start us, length us, event | category | flops | bytes accessed | tf_op | source)
XLA Modules:
  0.0 473.8 jit_solution(3291761606591850008)
XLA Ops:
  7.2 0.0 all-gather.3.cloned.1.call-start
  7.2 7.9 %fusion = (bf16[896,1536]{1,0:T(8,128)(2,1)}, f32[896,1536]{1,0:T(8,128)}) fusion(bf16[896,1536]{1,0:T(8,128)(2,1)} %param.2, f32[896,1536]{1,0:T(8,128)} %param.3), kind=kLoop, calls=%fused_computation.2 | loop fusion | flops 8257536 | bytes 16515072 | tf_op jit(solution)/shard_map/convert_element_type | solution.py:276
  15.1 0.0 copy-start
  15.1 0.0 all-gather.3.cloned.1.call-update
  15.1 0.0 all-gather.5.cloned.1.call-start
  15.2 1.7 copy-done
  16.9 4.2 convolution_convert_fusion
  21.0 70.1 %all-gather.3.cloned.1.call-done = bf16[3584,1536]{1,0:T(8,128)(2,1)} async-done(((bf16[896,1536]{1,0:T(8,128)(2,1)}), bf16[3584,1536]{1,0:T(8,128)(2,1)}) %all-gather.3.cloned.1.call-update) | async-done | bytes 11010064 | tf_op jit(solution)/shard_map/all_gather | solution.py:281
  91.2 4.8 %fusion.7 = bf16[896,896]{1,0:T(8,128)(2,1)S(1)} fusion(bf16[896,1536]{1,0:T(8,128)(2,1)S(1)} %copy-done, bf16[3584,1536]{1,0:T(8,128)(2,1)} %all-gather.3.cloned.1.call-done, s32[]{:T(128)S(6)} %select_n.37), kind=kOutput, calls=%fused_computation.11 | convolution fusion | flops 2467053568 | bytes 7110660 | tf_op jit(solution)/shard_map/dot_general | solution.py:21
  96.0 0.0 copy-start.1
  96.0 3.9 fusion.10
  99.9 0.0 copy-done.1
  99.9 7.5 %pad_maximum_fusion = bf16[2240,896]{1,0:T(8,128)(2,1)S(1)} fusion(bf16[448,896]{1,0:T(8,128)(2,1)S(1)} %fusion.10, bf16[896,896]{1,0:T(8,128)(2,1)S(1)} %fusion.7, bf16[896,896]{1,0:T(8,128)(2,1)S(1)} %copy-done.1), kind=kLoop, calls=%fused_computation.3 | loop fusion | flops 12042240 | bytes 8028160 | tf_op jit(solution)/shard_map/concatenate | solution.py:297
  107.5 55.3 %ring_sum.1 = bf16[280,896]{1,0:T(8,128)(2,1)} custom-call(bf16[8,280,896]{2,1,0:T(8,128)(2,1)S(1)} %bitcast.8), custom_call_target="tpu_custom_call" | custom-call | tf_op jit(solution)/shard_map/ring_sum/pallas_call | solution.py:258
  162.8 0.0 all-gather.5.cloned.1.call-update
  162.8 3.6 constant_dynamic-slice_fusion.x_ref
  166.4 105.0 %all-gather.5.cloned.1.call-done.shares_ref = bf16[8960,896]{1,0:T(8,128)(2,1)} async-done(((bf16[280,896]{1,0:T(8,128)(2,1)}), bf16[8960,896]{1,0:T(8,128)(2,1)}) %all-gather.5.cloned.1.call-update) | async-done | bytes 16056336 | tf_op jit(solution)/shard_map/all_gather | solution.py:303
  271.4 157.5 %chain.1 = bf16[3584,384]{1,0:T(8,128)(2,1)} custom-call(bf16[8960,896]{1,0:T(8,128)(2,1)} %all-gather.5.cloned.1.call-done.shares_ref, bf16[3584,384]{1,0:T(8,128)(2,1)} %constant_dynamic-slice_fusion.x_ref), custom_call_target="tpu_custom_call" | custom-call | tf_op jit(solution)/shard_map/chain/pallas_call | solution.py:156
  428.8 36.3 %all_to_all.19 = bf16[4,896,384]{2,1,0:T(8,128)(2,1)S(1)} all-to-all(bf16[4,896,384]{2,1,0:T(8,128)(2,1)} %bitcast.10), channel_id=1, replica_groups=mesh['row'=4,'col'=8] {'row'}, dimensions={0} | all-to-all | bytes 5505024 | tf_op jit(solution)/shard_map/all_to_all | solution.py:312
  465.2 1.8 copy.5
Async XLA Ops:
  7.2 84.0 %all-gather.3.cloned.1.call-start = ((), (), s32[]{:S(2)}) async-start(), calls=%async_computation.1 | async-start | bytes 13762560 | tf_op jit(solution)/shard_map/all_gather | solution.py:281
  15.1 1.8 copy-start
  15.1 256.2 %all-gather.5.cloned.1.call-start = ((), (), s32[]{:S(2)}) async-start(), calls=%async_computation.2 | async-start | bytes 16558080 | tf_op jit(solution)/shard_map/all_gather | solution.py:303
  96.0 4.0 copy-start.1
Sparse Core Ops, SparseCore 0:
  15.2 75.8 all-gather.2
  162.9 108.4 all-gather.4
